TPU v7x, 128 devices: a whole 4x4x4 slice. The times are simulated.
128 devices in a mesh: seq: 8 (over x, core), tensor: 8 (over z, y_lo), dp: 2 (over y_hi).
Axes of the slice: x: 4, y: 4 (y_hi: 2, y_lo: 2; y = y_hi * 2 + y_lo), z: 4, core: 2. Of those that a mesh axis runs over, the one named last changes fastest.
Arguments:
- ssm_input: bfloat16 [2, 2048, 8192], P('dp', 'seq', 'tensor'), may hold values from -6 to 6
- b_input: bfloat16 [2, 2048, 1024], P('dp', 'seq', 'tensor'), may hold values from -0.125 to 0.125
- c_input: bfloat16 [2, 2048, 1024], P('dp', 'seq', 'tensor'), may hold values from -0.125 to 0.125
- step_size: float32 [2, 128, 2048], P('dp', 'tensor', 'seq'), may hold values from 0 to 2048, as said below
- decay_rate: float32 [128], P('tensor'), may hold values from 0 to 1, as said below
- skip_gain: float32 [128], P('tensor'), may hold values from 0.5 to 2
- resets: int32 [2, 8], P('dp', 'seq'), may hold values 0 or 1
- out_grad: bfloat16 [2, 2048, 4096], P('dp', 'seq'), may hold values from -6 to 6
- out_weight: bfloat16 [4096, 8192], P(('seq', 'dp'), 'tensor'), may hold values from -0.0625 to 0.0625
Outputs:
- grad_input: bfloat16 [2, 2048, 8192], P('dp', 'seq', 'tensor')
- grad_b: float32 [2, 2048, 1024], P('dp', 'seq', 'tensor')
- grad_c: float32 [2, 2048, 1024], P('dp', 'seq', 'tensor')
- grad_weight: float32 [4096, 8192], P(('seq', 'dp'), 'tensor')
Inputs may be any that keep to these rules, and one draw needn't show every extreme that they name: `step_size`: positive per-position steps. `decay_rate`: positive per-head rates.
All inputs are finite; a program needn't handle non-finite values. No bound on the sum of `resets` on one device may be relied on, other than what follows from the above.
Results may differ from a plain program's by a relative error of at most 0.017.
Values may be sent and summed in bfloat16 or wider, within the bound.
A program may use at most 128 MiB of HBM per device.

v0:
```python
import jax
import jax.numpy as jnp
from jax import lax
from jax.sharding import PartitionSpec as P

P_SIZE = 64
N = 128
Q = 256


def prefix(value, axis, join, neutral, backward):
    count, mine = (lax.axis_size(axis), lax.axis_index(axis))
    pieces = jax.tree.map(lambda part: lax.all_gather(part, axis), value)
    if backward:
        pieces = jax.tree.map(lambda part: part[::-1], pieces)
        mine = count - 1 - mine
    running = jax.tree.map(
        lambda part, zero: jnp.full_like(part, 0) + jnp.asarray(zero, part.dtype), value, neutral
    )

    def step(position, running):
        longer = join(running, jax.tree.map(lambda part: part[position], pieces))
        return jax.tree.map(lambda new, old: jnp.where(position < mine, new, old), longer, running)

    return lax.fori_loop(0, count - 1, step, running)


def contract(pattern, former, latter):
    return jnp.einsum(pattern, former, latter, preferred_element_type=jnp.float32)


def block_tables(step_rows, head_rates):
    log_decay = jnp.cumsum(-step_rows * head_rates[..., None], axis=-1)
    last_log = log_decay[..., -1:]
    damping = jnp.exp(last_log[..., 0])
    to_end = jnp.moveaxis(jnp.exp(last_log - log_decay), -1, 0)[..., None]
    from_start = jnp.moveaxis(jnp.exp(log_decay), -1, 0)[..., None]
    positions = jnp.arange(log_decay.shape[-1])
    causal = positions[:, None] >= positions[None, :]
    spread = log_decay[..., :, None] - log_decay[..., None, :]
    weights = jnp.where(causal, jnp.exp(jnp.minimum(spread, 0.0)), 0.0)
    return (damping, to_end, from_start, weights)


def block_sums(inputs, b_rows, c_rows, grad_rows, to_end, from_start):
    weighted_in = (inputs.astype(jnp.float32) * to_end).astype(jnp.bfloat16)
    weighted_grad = (grad_rows.astype(jnp.float32) * from_start).astype(jnp.bfloat16)
    carried = contract("qgkp,qgn->gkpn", weighted_in, b_rows)
    adjoint = contract("qgkp,qgn->gkpn", weighted_grad, c_rows)
    return (carried, adjoint, weighted_in, weighted_grad)


def block_grads(
    inputs,
    b_rows,
    c_rows,
    grad_rows,
    skip_rows,
    to_end,
    from_start,
    weights,
    weighted_in,
    weighted_grad,
    state_in,
    adjoint_out,
):
    scores = contract("ign,jgn->gij", c_rows, b_rows)
    mixing = (weights * scores[:, None]).astype(jnp.bfloat16)
    skip_term = skip_rows[None, :, :, None]
    output = (
        contract("gkij,jgkp->igkp", mixing, inputs)
        + from_start * contract("gkpn,ign->igkp", state_in, c_rows)
        + skip_term * inputs.astype(jnp.float32)
    )
    grad_in = (
        contract("gkij,igkp->jgkp", mixing, grad_rows)
        + to_end * contract("gkpn,jgn->jgkp", adjoint_out, b_rows)
        + skip_term * grad_rows.astype(jnp.float32)
    )
    products = contract("igkp,jgkp->gkij", grad_rows, inputs)
    paired = (weights * products).astype(jnp.bfloat16)
    grad_b = contract("gkij,ign->jgn", paired, c_rows) + contract(
        "jgkp,gkpn->jgn", weighted_in, adjoint_out
    )
    grad_c = contract("gkij,jgn->ign", paired, b_rows) + contract(
        "igkp,gkpn->ign", weighted_grad, state_in
    )
    return (output.astype(jnp.bfloat16), grad_in.astype(jnp.bfloat16), grad_b, grad_c)


def forward_step(running, sliced):
    kept, carried, damping = sliced
    state_in = kept * running
    return (damping[..., None, None] * state_in + carried, state_in)


def backward_step(running, sliced):
    kept, adjoint, damping = sliced
    return (kept * (damping[..., None, None] * running + adjoint), running)


def compose(earlier, following):
    return (earlier[0] * following[0], following[0][..., None, None] * earlier[1] + following[1])


def body(
    ssm_input, b_input, c_input, step_size, decay_rate, skip_gain, resets, out_grad, out_weight
):
    head_count = decay_rate.shape[0]
    length = ssm_input.shape[1]
    blocks = length // Q
    incoming = out_grad[0]
    columns = incoming
    head_total = jnp.dot(
        columns,
        lax.all_gather(out_weight, ("seq", "dp"), axis=0, tiled=True),
        preferred_element_type=jnp.float32,
    )
    head_grad = head_total.astype(jnp.bfloat16)
    inputs = ssm_input[0].reshape(blocks, Q, 1, head_count, P_SIZE)
    b_rows = b_input[0].reshape(blocks, Q, 1, N)
    c_rows = c_input[0].reshape(blocks, Q, 1, N)
    grad_rows = head_grad.reshape(blocks, Q, 1, head_count, P_SIZE)
    step_rows = step_size[0].reshape(1, head_count, blocks, Q).transpose(2, 0, 1, 3)
    head_rates = decay_rate.reshape(1, head_count)
    skip_rows = skip_gain.reshape(1, head_count)
    keep_rows = (1 - resets[0]).astype(jnp.float32)
    decays, to_end, from_start, weights = jax.vmap(block_tables, in_axes=(0, None))(
        step_rows, head_rates
    )
    carried, adjoint, weighted_in, weighted_grad = jax.vmap(block_sums)(
        inputs, b_rows, c_rows, grad_rows, to_end, from_start
    )
    zero_state = jnp.zeros((1, head_count, P_SIZE, N), jnp.float32)
    local_out, local_states = lax.scan(forward_step, zero_state, (keep_rows, carried, decays))
    local_back, local_adjoints = lax.scan(
        backward_step, zero_state, (keep_rows, adjoint, decays), reverse=True
    )
    factors = keep_rows[:, None, None] * decays
    through = jnp.prod(factors, axis=0)
    unit_gain = jnp.ones_like(through)
    through_before, state_before = prefix(
        (through, local_out), "seq", compose, (unit_gain, zero_state), False
    )
    through_after, adjoint_after = prefix(
        (through, local_back), "seq", compose, (unit_gain, zero_state), True
    )
    final_state, states = lax.scan(forward_step, state_before, (keep_rows, carried, decays))
    final_adjoint, adjoints = lax.scan(
        backward_step, adjoint_after, (keep_rows, adjoint, decays), reverse=True
    )
    output, grad_in, grad_b, grad_c = jax.vmap(
        block_grads, in_axes=(0, 0, 0, 0, None, 0, 0, 0, 0, 0, 0, 0)
    )(
        inputs,
        b_rows,
        c_rows,
        grad_rows,
        skip_rows,
        to_end,
        from_start,
        weights,
        weighted_in,
        weighted_grad,
        states.astype(jnp.bfloat16),
        adjoints.astype(jnp.bfloat16),
    )
    outputs = output.reshape(length, head_count * P_SIZE)
    columns = incoming
    grad_weight = lax.psum_scatter(
        jnp.einsum("ld,lh->dh", columns, outputs, preferred_element_type=jnp.float32).astype(
            jnp.bfloat16
        ),
        ("seq", "dp"),
        scatter_dimension=0,
        tiled=True,
    ).astype(jnp.float32)
    return (
        grad_in.reshape(1, length, head_count * P_SIZE),
        grad_b.reshape(1, length, N),
        grad_c.reshape(1, length, N),
        grad_weight,
    )


def solution(mesh):
    in_specs = (
        P("dp", "seq", "tensor"),
        P("dp", "seq", "tensor"),
        P("dp", "seq", "tensor"),
        P("dp", "tensor", "seq"),
        P("tensor"),
        P("tensor"),
        P("dp", "seq"),
        P("dp", "seq", None),
        P(("seq", "dp"), "tensor"),
    )
    out_specs = (
        P("dp", "seq", "tensor"),
        P("dp", "seq", "tensor"),
        P("dp", "seq", "tensor"),
        P(("seq", "dp"), "tensor"),
    )
    return jax.shard_map(body, mesh=mesh, in_specs=in_specs, out_specs=out_specs, check_vma=False)
```

profile of v0, /device:TPU:1, one launch (start us, length us, event | category | flops | bytes accessed | tf_op | source)
XLA Modules:
  0.0 289.9 jit_solution(8070474870886657349)
XLA Ops:
  7.2 0.9 neg.15
  8.1 0.7 copy_multiply_fusion
  11.7 1.3 copy.106
  13.0 0.8 copy-done.2
  13.9 1.9 convolution_add_fusion
  15.9 0.7 all-gather.7.cloned.1.call-update
  16.6 0.6 copy.95
  17.2 0.7 copy.100
  18.0 12.0 %all-gather = f32[8,1,16,1]{2,3,1,0:T(1,128)S(1)} all-gather(f32[1,1,16,1]{2,3,1,0:T(1,128)} %get-tuple-element.390), channel_id=2, replica_groups=mesh['seq'=8,'tensor'=8,'dp'=2] {'seq'}, dimensions={0}, use_global_device_ids=true | all-gather | bytes 576 | tf_op jit(solution)/shard_map/all_gather | solution.py:13
  30.0 0.8 bitcast_add_fusion.2
  30.8 0.9 fusion.40
  31.7 20.0 %all-gather.11.cloned.1.call-done = f32[128,64,128]{2,1,0:T(8,128)} async-done(((f32[16,64,128]{2,1,0:T(8,128)}), f32[128,64,128]{2,1,0:T(8,128)}) %all-gather.11.cloned.1.call-update) | async-done | bytes 4194320 | tf_op jit(solution)/shard_map/all_gather | solution.py:13
  51.7 8.5 %while.19 = (s32[]{:T(128)}, f32[1,16,64,128]{3,2,1,0:T(8,128)S(1)}, s32[]{:T(128)}, f32[8,1,16]{2,1,0:T(1,128)S(1)}, f32[8,1,16,64,128]{4,3,2,1,0:T(8,128)}, /*index=5*/s32[]{:T(128)}, s32[]{:T(128)}) while((s32[]{:T(128)}, f32[1,16,64,128]{3,2,1,0:T(8,128)S(1)}, s32[]{:T(128)}, f32[8,1,16]{2,1,0:T(1,128)S(1)}, ...), condition=%wide.region_6.7_spmd.clone, body=%wide.region_5.6_spmd.clone.sunk | while | flops 524292 | bytes 1573161 | solution.py:25
  51.7 1.2 fusion.61
  52.9 1.2 fusion.61
  54.1 1.2 fusion.61
  55.3 1.2 fusion.61
  56.5 1.2 fusion.61
  57.8 1.2 fusion.61
  59.0 1.2 fusion.61
  60.5 2.5 fusion.21
  63.0 5.7 %convert_bitcast_fusion = bf16[4096,1024]{0,1:T(8,128)(2,1)} fusion(bf16[256,1024]{0,1:T(8,128)(2,1)S(1)} %bitcast.203, bf16[1,256,4096]{2,1,0:T(8,128)(2,1)S(1)} %copy-done), kind=kOutput, calls=%fused_computation.6 | convolution fusion | flops 2151677952 | bytes 11010048 | tf_op jit(solution)/shard_map/ld,lh->dh/dot_general | solution.py:171
  69.0 1.1 mul.273
  70.0 2.6 copy.101
  72.6 54.2 %all-gather.7.cloned.1.call-done = bf16[4096,1024]{1,0:T(8,128)(2,1)} async-done(((bf16[256,1024]{1,0:T(8,128)(2,1)}), bf16[4096,1024]{1,0:T(8,128)(2,1)}) %all-gather.7.cloned.1.call-update) | async-done | bytes 8388624 | tf_op jit(solution)/shard_map/all_gather | solution.py:116
  126.8 7.0 %multiply_convert_fusion.20 = (bf16[256,1024]{1,0:T(8,128)(2,1)}, bf16[256,1024]{1,0:T(8,128)(2,1)}) fusion(f32[256,1024]{1,0:T(8,128)} %copy.101, bf16[4096,1024]{1,0:T(8,128)(2,1)} %all-gather.7.cloned.1.call-done, bf16[1,256,4096]{2,1,0:T(8,128)(2,1)S(1)} %copy-done), kind=kOutput, calls=%fused_computation.44 | convolution fusion | flops 2148532224 | bytes 12582912 | tf_op jit(solution)/shard_map/dot_general | solution.py:114
  133.8 1.2 copy.102
  135.1 1.1 fusion.22
  136.3 2.2 copy.93
  138.5 2.3 copy.105
  140.7 1.5 convolution_bitcast_fusion.2
  142.2 2.8 convert_reduce_fusion
  145.0 0.8 fusion.26
  145.8 84.1 %reduce-scatter.2.cloned.1.call-done = bf16[256,1024]{0,1:T(8,128)(2,1)} async-done(((bf16[4096,1024]{0,1:T(8,128)(2,1)}), bf16[256,1024]{0,1:T(8,128)(2,1)}) %reduce-scatter.2.cloned.1.call-update) | async-done | bytes 524304 | tf_op jit(solution)/shard_map/reduce_scatter | solution.py:170
  230.0 2.2 copy.113
  232.2 32.5 %all-gather.9.cloned.1.call-done = f32[128,64,128]{2,1,0:T(8,128)} async-done(((f32[16,64,128]{2,1,0:T(8,128)}), f32[128,64,128]{2,1,0:T(8,128)}) %all-gather.9.cloned.1.call-update) | async-done | bytes 4194320 | tf_op jit(solution)/shard_map/all_gather | solution.py:13
  264.6 4.9 %rev.7 = f32[8,1,16,64,128]{4,3,2,1,0:T(8,128)} reverse(f32[8,1,16,64,128]{4,3,2,1,0:T(8,128)} %bitcast.191), dimensions={0} | reverse | bytes 8388608 | tf_op jit(solution)/shard_map/rev | solution.py:15
  269.5 8.5 %while.18 = (s32[]{:T(128)}, f32[1,16,64,128]{3,2,1,0:T(8,128)S(1)}, s32[]{:T(128)}, f32[8,1,16]{2,1,0:T(1,128)S(1)}, f32[8,1,16,64,128]{4,3,2,1,0:T(8,128)}, /*index=5*/s32[]{:T(128)}, s32[]{:T(128)}) while((s32[]{:T(128)}, f32[1,16,64,128]{3,2,1,0:T(8,128)S(1)}, s32[]{:T(128)}, f32[8,1,16]{2,1,0:T(1,128)S(1)}, ...), condition=%wide.region_3.4_spmd.clone, body=%wide.region_2.3_spmd.clone.sunk | while | flops 524292 | bytes 1573161 | solution.py:25
  269.5 1.2 fusion.60
  270.8 1.2 fusion.60
  272.0 1.2 fusion.60
  273.2 1.2 fusion.60
  274.4 1.2 fusion.60
  275.6 1.2 fusion.60
  276.8 1.2 fusion.60
  278.7 2.8 fusion.20
  281.4 1.0 copy.112
  282.4 0.9 fusion.24
  (66 shorter events, 3.8 us)
Async XLA Ops:
  7.2 55.8 %copy-start = (bf16[1,256,4096]{2,1,0:T(8,128)(2,1)S(1)}, bf16[1,256,4096]{2,1,0:T(8,128)(2,1)}, u32[]{:S(2)}) copy-start(bf16[1,256,4096]{2,1,0:T(8,128)(2,1)} %param.20) | copy-start | bytes 6291460
  7.2 23.6 %copy-start.5 = (bf16[1,256,128]{2,1,0:T(8,128)(2,1)S(1)}, bf16[1,256,128]{2,1,0:T(8,128)(2,1)}, u32[]{:S(2)}) copy-start(bf16[1,256,128]{2,1,0:T(8,128)(2,1)} %param.14) | copy-start | bytes 196612
  7.2 23.6 %copy-start.6 = (bf16[1,256,128]{2,1,0:T(8,128)(2,1)S(1)}, bf16[1,256,128]{2,1,0:T(8,128)(2,1)}, u32[]{:S(2)}) copy-start(bf16[1,256,128]{2,1,0:T(8,128)(2,1)} %param.15) | copy-start | bytes 196612
  7.2 44.5 %all-gather.11.cloned.1.call-start = ((), (), s32[]{:S(2)}) async-start(), calls=%async_computation.4 | async-start | bytes 4718592 | tf_op jit(solution)/shard_map/all_gather | solution.py:13
  12.9 47.6 %copy-start.4 = (bf16[1,256,1024]{1,2,0:T(8,128)(2,1)}, bf16[1,256,1024]{1,2,0:T(8,128)(2,1)S(1)}, u32[]{:S(2)}) copy-start(bf16[1,256,1024]{1,2,0:T(8,128)(2,1)S(1)} %copy.106) | copy-start | bytes 1572868
  13.0 0.8 copy-start.2
  15.8 111.0 %all-gather.7.cloned.1.call-start = ((), (), s32[]{:S(2)}) async-start(), calls=%async_computation.1 | async-start | bytes 8912896 | tf_op jit(solution)/shard_map/all_gather | solution.py:116
  16.6 213.4 %reduce-scatter.2.cloned.1.call-start = ((), (), s32[]{:S(2)}) async-start(), calls=%async_computation.2 | async-start | bytes 8912896 | tf_op jit(solution)/shard_map/reduce_scatter | solution.py:170
  30.0 112.2 %copy-start.8 = (pred[256,256]{1,0:T(8,128)(4,1)}, pred[256,256]{1,0:T(8,128)(4,1)S(1)}, u32[]{:S(2)}) copy-start(pred[256,256]{1,0:T(8,128)(4,1)S(1)} %iota_compare_fusion) | copy-start | bytes 196612
  30.8 111.4 %copy-start.9 = (f32[16,256]{1,0:T(8,128)}, f32[16,256]{1,0:T(8,128)S(1)}, u32[]{:S(2)}) copy-start(f32[16,256]{1,0:T(8,128)S(1)} %bitcast_add_fusion.2) | copy-start | bytes 49156
  30.8 29.4 %copy-start.7 = (f32[256,16]{0,1:T(8,128)S(1)}, f32[256,16]{0,1:T(8,128)}, u32[]{:S(2)}) copy-start(f32[256,16]{0,1:T(8,128)} %copy.100) | copy-start | bytes 49156
  51.7 8.8 %copy-start.11 = (f32[16]{0:T(128)S(1)}, f32[16]{0:T(128)}, u32[]{:S(2)}) copy-start(f32[16]{0:T(128)} %param.18) | copy-start | bytes 196
  68.7 195.9 %all-gather.9.cloned.1.call-start = ((), (), s32[]{:S(2)}) async-start(), calls=%async_computation.3 | async-start | bytes 4718592 | tf_op jit(solution)/shard_map/all_gather | solution.py:13
  72.6 62.5 %copy-start.10 = (f32[16]{0:T(128)S(1)}, f32[16]{0:T(128)}, u32[]{:S(2)}) copy-start(f32[16]{0:T(128)} %get-tuple-element.389) | copy-start | bytes 196
  135.1 1.1 copy-start.1
  269.5 8.8 %copy-start.3 = (bf16[1,256,1024]{1,2,0:T(8,128)(2,1)S(1)}, bf16[1,256,1024]{1,2,0:T(8,128)(2,1)}, u32[]{:S(2)}) copy-start(bf16[1,256,1024]{1,2,0:T(8,128)(2,1)} %copy-done.2) | copy-start | bytes 1572868
Sparse Core Ops, SparseCore 0:
  15.9 35.6 all-gather.10
  54.1 72.6 all-gather.6
  131.2 98.7 reduce-scatter.1
  232.1 32.4 all-gather.8
where the time goes:
time: 291 us; the launch traced here: 290 us
  waiting for transfers between devices  192 us (66%)
  matrix products  28.8 us (10%)
  local copies, waits for them, and re-layouts  21.4 us (7%)
  other arithmetic  20.7 us (7%)
  between operations  14.7 us (5%)
  blocking collectives  12 us (4%)
    reduce_scatter x1, waiting for transfers between devices, body(): lax.psum_scatter(jnp.einsum('ld,lh->dh', columns, outputs, preferred_elem...  84.1 us
    all_gather x1, waiting for transfers between devices, body(): lax.all_gather(out_weight, ('seq', 'dp'), axis=0, tiled=True)  54.2 us
    all_gather x2, waiting for transfers between devices, prefix(): pieces = jax.tree.map(lambda part: lax.all_gather(part, axis), value)  52.5 us
    select_n x14, other arithmetic, step(): jnp.where(position < mine, new, old)  16.5 us
    dot_general x12, matrix products, contract(): jnp.einsum(pattern, former, latter, preferred_element_type=jnp.float32)  16.1 us
    all_gather x1, blocking collectives, prefix(): pieces = jax.tree.map(lambda part: lax.all_gather(part, axis), value)  12 us
    dot_general x1, matrix products, body(): jnp.dot(columns, lax.all_gather(out_weight, ('seq', 'dp'), axis=0, tiled=...  7.02 us
  transfers between devices with their start and end apart: 4, of which 4 were waited for; matrix products, arithmetic and copies ran while one was open for 15% of the time, Pallas kernels for 0%

commit v1 on v0

v1 whole, which is shorter than its diff:
```python
import jax
import jax.numpy as jnp
from jax import lax
from jax.experimental import pallas as pl
from jax.experimental.pallas import tpu as pltpu
from jax.sharding import PartitionSpec as P

MESH = pl.DeviceIdType.MESH
BF = jnp.bfloat16
F32 = jnp.float32
Q, HEADS, PS, N = 256, 16, 64, 128
CH, HC, CW = 4, 4, 256
SUB = 2


def mm(a, b, ca=1, cb=0, precision=None):
    return lax.dot_general(
        a, b, (((ca,), (cb,)), ((), ())), preferred_element_type=F32, precision=precision
    )


def kernel(
    x_ref, b_ref, c_ref, step_ref, rate_ref, skip_ref, reset_ref, og_ref, w_ref,
    gin_ref, gb_ref, gc_ref, gw_ref,
    wb, oga, ogs, ogt, xm, mix, wt, ee, te, win, wg, car, fin, fout, stt,
    yi, outs, hp, hs, hr, gg, adl, ain, aout, adt, gi,
    ds, dr, dx, dxr, rowbuf, colbuf, psum,
    loc_sem, ogl_sem, w_send, w_recv, wc_send, wc_recv, oy_send, oy_recv, oz_send, oz_recv,
    f_send, f_recv, a_send, a_recv, o_send, o_recv, h_send, h_recv,
    dc_send, dc_recv, dx_send, dx_recv,
):
    s, t, d = lax.axis_index("seq"), lax.axis_index("tensor"), lax.axis_index("dp")
    x, core = s // 2, lax.rem(s, 2)
    z, yl = t // 2, lax.rem(t, 2)

    def xdev(r):
        return (lax.rem(x + r, 4) * 2 + core, t, d)

    def zdev(r):
        return (s, lax.rem(z + r, 4) * 2 + yl, d)

    twin = (x * 2 + 1 - core, t, d)
    partner = (s, t, 1 - d)
    nxt = (lax.rem(s + 1, 8), t, d)
    prv = (lax.rem(s + 7, 8), t, d)

    bar = pltpu.get_barrier_semaphore()
    peers = [xdev(1), xdev(2), xdev(3), zdev(1), zdev(2), zdev(3), twin, partner, nxt, prv]
    for p in peers:
        pl.semaphore_signal(bar, inc=1, device_id=p, device_id_type=MESH)
    pl.semaphore_wait(bar, len(peers))

    def remote(src, dst, ssem, rsem, dev):
        return pltpu.make_async_remote_copy(
            src_ref=src, dst_ref=dst, send_sem=ssem, recv_sem=rsem, device_id=dev, device_id_type=MESH
        )

    def cols(c):
        return pl.ds(c * CW, CW)

    ogl = []
    for k in range(8):
        cp = pltpu.make_async_copy(
            og_ref.at[pl.ds(z * 64, 64), pl.ds((2 * k + 1 - d) * 256, 256)],
            ogs.at[:, pl.ds(k * 256, 256)], ogl_sem.at[0, k])
        cp.start()
        ogl.append(cp)
    wsends = []
    for c in range(CH):
        for r in (1, 3, 2):
            cp = remote(w_ref.at[:, cols(c)], wb.at[c, s], w_send.at[c, r - 1], w_recv.at[c, r - 1], xdev(r))
            cp.start()
            wsends.append(cp)
        cp = remote(w_ref.at[:, cols(c)], wb.at[c, s], wc_send.at[c, 0], wc_recv.at[c, 0], twin)
        cp.start()
        wsends.append(cp)
    for cp in ogl:
        cp.wait()
    RS = 64 // SUB

    def ogrows(zz, u):
        return pl.ds(Q + zz * 64 + u * RS, RS)

    oysends = []
    for u in range(SUB):
        cp = remote(ogs.at[pl.ds(u * RS, RS), :], oga.at[ogrows(z, u), :], oy_send.at[u], oy_recv.at[u], partner)
        cp.start()
        oysends.append(cp)
    locs = []
    for c in range(CH):
        cp = pltpu.make_async_copy(w_ref.at[:, cols(c)], wb.at[c, s], loc_sem.at[c])
        cp.start()
        locs.append(cp)
    for k in range(8):
        cp = pltpu.make_async_copy(
            og_ref.at[:, pl.ds((2 * k + d) * 256, 256)], oga.at[pl.ds(0, Q), pl.ds(k * 256, 256)], ogl_sem.at[1, k])
        cp.start()
        locs.append(cp)

    rate = rate_ref[...]
    eye = lax.broadcasted_iota(jnp.int32, (HEADS, HEADS), 0) == lax.broadcasted_iota(jnp.int32, (HEADS, HEADS), 1)
    rate_col = jnp.sum(jnp.where(eye, jnp.broadcast_to(rate, (HEADS, HEADS)), 0.0), axis=1, keepdims=True)
    run = -step_ref[...] * rate_col
    lane = lax.broadcasted_iota(jnp.int32, (HEADS, Q), 1)
    for k in range(8):
        run = run + jnp.where(lane >= (1 << k), pltpu.roll(run, 1 << k, 1), 0.0)
    rowbuf[...] = jnp.zeros_like(rowbuf)
    rowbuf[0:HEADS, :] = run
    lcol = jnp.transpose(rowbuf[...])
    colbuf[...] = lcol
    hrow = lax.broadcasted_iota(jnp.int32, (128, HEADS * PS), 0)
    hcol = lax.broadcasted_iota(jnp.int32, (128, HEADS * PS), 1) // PS
    spread = jnp.where(hrow == hcol, 1.0, 0.0).astype(F32)
    hi = lax.Precision.HIGHEST
    ee[...] = mm(jnp.exp(lcol), spread, precision=hi)
    te[...] = mm(jnp.exp(lcol[Q - 1 : Q, :] - lcol), spread, precision=hi)
    skip_row = mm(jnp.broadcast_to(skip_ref[...], (8, HEADS)), spread[0:HEADS, :], precision=hi)[0:1, :]
    keep = (1 - reset_ref[0, 0]).astype(F32)

    bm, cm = b_ref[...], c_ref[...]
    win[...] = (x_ref[...].astype(F32) * te[...]).astype(BF)
    car[...] = mm(bm, win[...], 0, 0)

    def decay(c):
        return ee[Q - 1 : Q, cols(c)]

    def forward_step(c):
        @pl.when(s == 0)
        def _():
            stt[c] = jnp.zeros((N, CW), BF)
            fout[c] = car[:, cols(c)]

        @pl.when(s > 0)
        def _():
            remote(fout.at[c], fin.at[c], f_send.at[c], f_recv.at[c], nxt).wait_recv()
            state = keep * fin[c]
            stt[c] = state.astype(BF)
            fout[c] = decay(c) * state + car[:, cols(c)]

        @pl.when(s < 7)
        def _():
            remote(fout.at[c], fin.at[c], f_send.at[c], f_recv.at[c], nxt).start()

    scores = mm(cm, bm, 1, 1)
    ii = lax.broadcasted_iota(jnp.int32, (Q, Q), 0)
    jj = lax.broadcasted_iota(jnp.int32, (Q, Q), 1)
    causal = ii >= jj
    mlane = lax.broadcasted_iota(jnp.int32, (1, CW), 1) // PS
    masks = [jnp.where(mlane == k, 1.0, 0.0).astype(BF) for k in range(HC)]

    def intra(c):
        xc = x_ref[:, cols(c)]
        for k in range(HC):
            h = c * HC + k
            gap = colbuf[:, h : h + 1] - rowbuf[h : h + 1, :]
            w = jnp.where(causal, jnp.exp(jnp.minimum(gap, 0.0)), 0.0)
            wt[h] = w
            mix[h] = (w * scores).astype(BF)
            xm[c, k * Q : (k + 1) * Q, :] = xc * masks[k]
        acc = skip_row[:, c * CW : (c + 1) * CW] * xc.astype(F32)
        for k in range(HC):
            acc = acc + mm(mix[c * HC + k], xm[c, k * Q : (k + 1) * Q, :])
        yi[:, cols(c)] = acc

    ozsends = []

    def share_og(u):
        remote(ogs.at[pl.ds(u * RS, RS), :], oga.at[ogrows(z, u), :], oy_send.at[u], oy_recv.at[u], partner).wait_recv()
        for r in (1, 3, 2):
            piece = oga.at[ogrows(z, u), :]
            cp = remote(piece, piece, oz_send.at[r - 1, u], oz_recv.at[r - 1, u], zdev(r))
            cp.start()
            ozsends.append(cp)

    intra(0)
    intra(1)
    share_og(0)
    intra(2)
    share_og(1)
    intra(3)

    osends = []

    def output(c):
        o = yi[:, cols(c)] + ee[:, cols(c)] * mm(cm, stt[c])
        outs[c, 0:Q, :] = o.astype(BF)
        cp = remote(outs.at[c, pl.ds(0, Q), :], outs.at[c, pl.ds(Q, Q), :], o_send.at[c], o_recv.at[c], partner)
        cp.start()
        osends.append(cp)

    fsends = []

    def share_w(c):
        for r in (1, 3, 2):
            frm = lax.rem(x + 4 - r, 4) * 2 + core
            remote(w_ref.at[:, cols(c)], wb.at[c, frm], w_send.at[c, r - 1], w_recv.at[c, r - 1], xdev(r)).wait_recv()
            cp = remote(wb.at[c, frm], wb.at[c, frm], wc_send.at[c, r], wc_recv.at[c, r], twin)
            cp.start()
            fsends.append(cp)

    hsends = []

    def head(c):
        for r in range(4):
            frm = lax.rem(x + 4 - r, 4) * 2 + 1 - core
            remote(wb.at[c, frm], wb.at[c, frm], wc_send.at[c, r], wc_recv.at[c, r], twin).wait_recv()
        wmat = wb[c].reshape(8 * 256, CW)
        hs[c] = mm(oga[Q : 2 * Q, :], wmat).astype(BF)
        cp = remote(hs.at[c], hr.at[c], h_send.at[c], h_recv.at[c], partner)
        cp.start()
        hsends.append(cp)
        hp[c] = mm(oga[0:Q, :], wmat)

    def head_grad(c):
        remote(hs.at[c], hr.at[c], h_send.at[c], h_recv.at[c], partner).wait_recv()
        g = (hp[c] + hr[c].astype(F32)).astype(BF)
        gg[:, cols(c)] = g
        wgc = (g.astype(F32) * ee[:, cols(c)]).astype(BF)
        wg[:, cols(c)] = wgc
        adl[c] = mm(cm, wgc, 0, 0)

    def backward_step(c):
        @pl.when(s == 7)
        def _():
            adt[c] = jnp.zeros((N, CW), BF)
            aout[c] = keep * adl[c]

        @pl.when(s < 7)
        def _():
            remote(aout.at[c], ain.at[c], a_send.at[c], a_recv.at[c], prv).wait_recv()
            back = ain[c]
            adt[c] = back.astype(BF)
            aout[c] = keep * (decay(c) * back + adl[c])

        @pl.when(s > 0)
        def _():
            remote(aout.at[c], ain.at[c], a_send.at[c], a_recv.at[c], prv).start()

    def within_grads(c):
        gc = gg[:, cols(c)]
        prod = mm(gc, xm[c], 1, 1)
        acc = skip_row[:, c * CW : (c + 1) * CW] * gc.astype(F32)
        tot = None
        for k in range(HC):
            h = c * HC + k
            paired = (wt[h] * prod[:, k * Q : (k + 1) * Q]).astype(BF).astype(F32)
            tot = paired if tot is None else tot + paired
            acc = acc + mm(mix[h], gc * masks[k], 0, 0)
        psum[...] = tot if c == 0 else psum[...] + tot
        gi[:, cols(c)] = acc

    def finish(c):
        gin_ref[:, cols(c)] = (gi[:, cols(c)] + te[:, cols(c)] * mm(bm, adt[c])).astype(BF)
        nb = mm(win[:, cols(c)], adt[c], 1, 1)
        nc = mm(wg[:, cols(c)], stt[c], 1, 1)
        gb_ref[...] = nb if c == 0 else gb_ref[...] + nb
        gc_ref[...] = nc if c == 0 else gc_ref[...] + nc

    dcsends, dxsends = [], []

    def weight_partial(c):
        remote(outs.at[c, pl.ds(0, Q), :], outs.at[c, pl.ds(Q, Q), :], o_send.at[c], o_recv.at[c], partner).wait_recv()
        oc = outs[c]
        for r in (2, 1, 3, 0):
            other = lax.rem(x + r, 4) * 2 + 1 - core
            ds[c, r] = mm(ogt[other], oc).astype(BF)
            cp = remote(ds.at[c, r], dr.at[c, r], dc_send.at[c, r], dc_recv.at[c, r], twin)
            cp.start()
            dcsends.append(cp)

    def weight_send(c):
        oc = outs[c]
        for r in (2, 1, 3, 0):
            own = mm(ogt[lax.rem(x + r, 4) * 2 + core], oc)
            remote(ds.at[c, r], dr.at[c, r], dc_send.at[c, r], dc_recv.at[c, r], twin).wait_recv()
            both = own + dr[c, r].astype(F32)
            if r == 0:
                gw_ref[:, cols(c)] = both
            else:
                dx[c, r - 1] = both.astype(BF)
                cp = remote(dx.at[c, r - 1], dxr.at[c, r - 1], dx_send.at[c, r - 1], dx_recv.at[c, r - 1], xdev(r))
                cp.start()
                dxsends.append(cp)

    def weight_sum(c):
        tot = gw_ref[:, cols(c)]
        for r in range(1, 4):
            remote(dx.at[c, r - 1], dxr.at[c, r - 1], dx_send.at[c, r - 1], dx_recv.at[c, r - 1], xdev(r)).wait_recv()
            tot = tot + dxr[c, r - 1].astype(F32)
        gw_ref[:, cols(c)] = tot

    for c in range(CH):
        forward_step(c)
        output(c)
    for cp in locs:
        cp.wait()
    share_w(0)
    for r in (1, 2, 3):
        frm = lax.rem(z + 4 - r, 4)
        for u in range(SUB):
            piece = oga.at[ogrows(frm, u), :]
            remote(piece, piece, oz_send.at[r - 1, u], oz_recv.at[r - 1, u], zdev(r)).wait_recv()
    for k in range(8):
        ogt[k] = jnp.transpose(oga[:, k * 256 : (k + 1) * 256])
    head(0)
    share_w(1)
    head(1)
    weight_partial(0)
    share_w(2)
    head(2)
    weight_send(0)
    weight_partial(1)
    share_w(3)
    head(3)
    head_grad(0)
    weight_send(1)
    backward_step(0)
    head_grad(1)
    weight_partial(2)
    backward_step(1)
    head_grad(2)
    weight_send(2)
    backward_step(2)
    weight_partial(3)
    head_grad(3)
    weight_send(3)
    backward_step(3)
    for c in range(CH):
        within_grads(c)
        finish(c)
    pb = psum[...].astype(BF)
    gb_ref[...] = gb_ref[...] + mm(pb, cm, 0, 0)
    gc_ref[...] = gc_ref[...] + mm(pb, bm)
    for c in range(CH):
        weight_sum(c)

    for cp in wsends + oysends + ozsends + fsends + osends + hsends + dcsends + dxsends:
        cp.wait_send()
    for c in range(CH):

        @pl.when(s < 7)
        def _():
            remote(fout.at[c], fin.at[c], f_send.at[c], f_recv.at[c], nxt).wait_send()

        @pl.when(s > 0)
        def _():
            remote(aout.at[c], ain.at[c], a_send.at[c], a_recv.at[c], prv).wait_send()


def body(ssm_input, b_input, c_input, step_size, decay_rate, skip_gain, resets, out_grad, out_weight):
    vm, anym = pl.BlockSpec(memory_space=pltpu.VMEM), pl.BlockSpec(memory_space=pl.ANY)
    width = HEADS * PS
    dma = pltpu.SemaphoreType.DMA
    v = pltpu.VMEM
    scratch = [
        v((CH, 8, 256, CW), BF), v((2 * Q, 2048), BF), v((64, 2048), BF), v((8, 256, 2 * Q), BF),
        v((CH, HC * Q, CW), BF), v((HEADS, Q, Q), BF), v((HEADS, Q, Q), F32),
        v((Q, width), F32), v((Q, width), F32), v((Q, width), BF), v((Q, width), BF),
        v((N, width), F32), v((CH, N, CW), F32), v((CH, N, CW), F32), v((CH, N, CW), BF),
        v((Q, width), F32), v((CH, 2 * Q, CW), BF), v((CH, Q, CW), F32), v((CH, Q, CW), BF), v((CH, Q, CW), BF),
        v((Q, width), BF), v((CH, N, CW), F32), v((CH, N, CW), F32), v((CH, N, CW), F32), v((CH, N, CW), BF),
        v((Q, width), F32),
        v((CH, 4, 256, CW), BF), v((CH, 4, 256, CW), BF), v((CH, 3, 256, CW), BF), v((CH, 3, 256, CW), BF),
        v((128, Q), F32), v((Q, 128), F32), v((Q, Q), F32),
        dma((CH,)), dma((2, 8)), dma((CH, 3)), dma((CH, 3)), dma((CH, 4)), dma((CH, 4)), dma((SUB,)), dma((SUB,)),
        dma((3, SUB)), dma((3, SUB)),
        dma((CH,)), dma((CH,)), dma((CH,)), dma((CH,)), dma((CH,)), dma((CH,)), dma((CH,)), dma((CH,)),
        dma((CH, 4)), dma((CH, 4)), dma((CH, 3)), dma((CH, 3)),
    ]
    gin, gb, gc, gw = pl.pallas_call(
        kernel,
        out_shape=(
            jax.ShapeDtypeStruct((Q, width), BF),
            jax.ShapeDtypeStruct((Q, N), F32),
            jax.ShapeDtypeStruct((Q, N), F32),
            jax.ShapeDtypeStruct((256, width), F32),
        ),
        in_specs=[vm, vm, vm, vm, vm, vm, pl.BlockSpec(memory_space=pltpu.SMEM), anym, anym],
        out_specs=(vm, vm, vm, vm),
        scratch_shapes=scratch,
        compiler_params=pltpu.CompilerParams(
            collective_id=0, has_side_effects=True, vmem_limit_bytes=60 * 2**20
        ),
        name="block_backward",
    )(
        ssm_input[0], b_input[0], c_input[0], step_size[0], decay_rate.reshape(1, HEADS),
        skip_gain.reshape(1, HEADS), resets, out_grad[0], out_weight,
    )
    return gin[None], gb[None], gc[None], gw


def solution(mesh):
    in_specs = (
        P("dp", "seq", "tensor"),
        P("dp", "seq", "tensor"),
        P("dp", "seq", "tensor"),
        P("dp", "tensor", "seq"),
        P("tensor"),
        P("tensor"),
        P("dp", "seq"),
        P("dp", "seq", None),
        P(("seq", "dp"), "tensor"),
    )
    out_specs = (
        P("dp", "seq", "tensor"),
        P("dp", "seq", "tensor"),
        P("dp", "seq", "tensor"),
        P(("seq", "dp"), "tensor"),
    )
    return jax.shard_map(body, mesh=mesh, in_specs=in_specs, out_specs=out_specs, check_vma=False)
```

time: 291 us -> 120 us (0.41)
  the two profiles are of different devices: /device:TPU:1 before, /device:TPU:18 now
where the time goes in v1:
time: 120 us
  Pallas kernels  113 us (94%)
  local copies, waits for them, and re-layouts  6.06 us (5%)
  between operations  1.3 us (1%)
    pallas_call x1, Pallas kernels, body(): pl.pallas_call(kernel, out_shape=(jax.ShapeDtypeStruct((Q, width), BF), j...  113 us
    unnamed x6, local copies, waits for them, and re-layouts  6.06 us

profile of v1, /device:TPU:18, one launch (start us, length us, event | category | flops | bytes accessed | tf_op | source)
XLA Modules:
  0.0 119.9 jit_solution(7320999387362497359)
XLA Ops:
  1.3 112.5 %block_backward.1 = (bf16[256,1024]{1,0:T(8,128)(2,1)}, f32[256,128]{1,0:T(8,128)}, f32[256,128]{1,0:T(8,128)}, f32[256,1024]{1,0:T(8,128)}) custom-call(bf16[256,1024]{1,0:T(8,128)(2,1)} %bitcast.11, bf16[256,128]{1,0:T(8,128)(2,1)} %bitcast.15, bf16[256,128]{1,0:T(8,128)(2,1)} %bitcast.16, f32[16,256]{1,0:T(8,128)} %bitcast.17, f32[1,16]{1,0:T(1,128)} %bitcast.18, ...), custom_call_target="tpu_custom_call" | custom-call | tf_op jit(solution)/shard_map/block_backward/pallas_call | solution.py:370
  113.8 0.0 copy-start
  113.8 2.0 %copy.18 = bf16[1,256,1024]{2,1,0:T(8,128)(2,1)} copy(bf16[1,256,1024]{2,1,0:T(8,128)(2,1)} %bitcast.12) | data formatting | bytes 1048576
  115.8 1.6 %copy.19 = f32[1,256,128]{2,1,0:T(8,128)} copy(f32[1,256,128]{2,1,0:T(8,128)} %bitcast.14) | data formatting | bytes 262144
  117.3 1.6 %copy.20 = f32[1,256,128]{2,1,0:T(8,128)} copy(f32[1,256,128]{2,1,0:T(8,128)} %bitcast.13) | data formatting | bytes 262144
  118.9 0.0 copy-done
  118.9 1.0 copy.21
Async XLA Ops:
  113.8 5.1 %copy-start = (f32[256,1024]{1,0:T(8,128)S(1)}, f32[256,1024]{1,0:T(8,128)}, u32[]{:S(2)}) copy-start(f32[256,1024]{1,0:T(8,128)} %get-tuple-element.19) | copy-start | bytes 3145732

commit v2 on v1

--- a/solution.py
+++ b/solution.py
@@ -22,12 +22,12 @@
 def kernel(
     x_ref, b_ref, c_ref, step_ref, rate_ref, skip_ref, reset_ref, og_ref, w_ref,
     gin_ref, gb_ref, gc_ref, gw_ref,
-    wb, oga, ogs, ogt, xm, mix, wt, ee, te, win, wg, car, fin, fout, stt,
-    yi, outs, hp, hs, hr, gg, adl, ain, aout, adt, gi,
-    ds, dr, dx, dxr, rowbuf, colbuf, psum,
-    loc_sem, ogl_sem, w_send, w_recv, wc_send, wc_recv, oy_send, oy_recv, oz_send, oz_recv,
-    f_send, f_recv, a_send, a_recv, o_send, o_recv, h_send, h_recv,
-    dc_send, dc_recv, dx_send, dx_recv,
+    wb, oga, ogs, ogt, xm, mix, wt, ee, te, win, wg, stt, adt, yi, outs, hp, hs, hr, gg, gi,
+    cx, cxr, fb, fbr, sacc, sx, al, alr, ab, abr, ax,
+    ds, dr, da, dar, dk, db, dbr, rowbuf, colbuf, psum,
+    loc_sem, ogl_sem, w_send, w_recv, wr_send, wr_recv, wc_send, wc_recv, oy_send, oy_recv, oz_send, oz_recv,
+    cx_send, cx_recv, f_send, f_recv, sx_send, sx_recv, al_send, al_recv, a_send, a_recv, ax_send, ax_recv,
+    o_send, o_recv, h_send, h_recv, dc_send, dc_recv, da_send, da_recv, db_send, db_recv,
 ):
     s, t, d = lax.axis_index("seq"), lax.axis_index("tensor"), lax.axis_index("dp")
     x, core = s // 2, lax.rem(s, 2)
@@ -41,11 +41,9 @@
 
     twin = (x * 2 + 1 - core, t, d)
     partner = (s, t, 1 - d)
-    nxt = (lax.rem(s + 1, 8), t, d)
-    prv = (lax.rem(s + 7, 8), t, d)
 
     bar = pltpu.get_barrier_semaphore()
-    peers = [xdev(1), xdev(2), xdev(3), zdev(1), zdev(2), zdev(3), twin, partner, nxt, prv]
+    peers = [xdev(1), xdev(2), xdev(3), zdev(1), zdev(2), zdev(3), twin, partner]
     for p in peers:
         pl.semaphore_signal(bar, inc=1, device_id=p, device_id_type=MESH)
     pl.semaphore_wait(bar, len(peers))
@@ -66,14 +64,20 @@
         cp.start()
         ogl.append(cp)
     wsends = []
-    for c in range(CH):
-        for r in (1, 3, 2):
-            cp = remote(w_ref.at[:, cols(c)], wb.at[c, s], w_send.at[c, r - 1], w_recv.at[c, r - 1], xdev(r))
+
+    def w_copy(c, r):
+        k = 0 if r == 1 else 1
+        return remote(w_ref.at[:, cols(c)], wb.at[c, s], w_send.at[c, k], w_recv.at[c, k], xdev(r))
+
+    def w_twin(c, j, frm):
+        return remote(wb.at[c, frm], wb.at[c, frm], wc_send.at[c, j], wc_recv.at[c, j], twin)
+
+    def send_w(c):
+        own = remote(w_ref.at[:, cols(c)], wb.at[c, s], wc_send.at[c, 0], wc_recv.at[c, 0], twin)
+        for cp in (w_copy(c, 1), w_copy(c, 3), own):
             cp.start()
             wsends.append(cp)
-        cp = remote(w_ref.at[:, cols(c)], wb.at[c, s], wc_send.at[c, 0], wc_recv.at[c, 0], twin)
-        cp.start()
-        wsends.append(cp)
+
     for cp in ogl:
         cp.wait()
     RS = 64 // SUB
@@ -86,6 +90,8 @@
         cp = remote(ogs.at[pl.ds(u * RS, RS), :], oga.at[ogrows(z, u), :], oy_send.at[u], oy_recv.at[u], partner)
         cp.start()
         oysends.append(cp)
+    send_w(0)
+    send_w(1)
     locs = []
     for c in range(CH):
         cp = pltpu.make_async_copy(w_ref.at[:, cols(c)], wb.at[c, s], loc_sem.at[c])
@@ -119,27 +125,109 @@
 
     bm, cm = b_ref[...], c_ref[...]
     win[...] = (x_ref[...].astype(F32) * te[...]).astype(BF)
-    car[...] = mm(bm, win[...], 0, 0)
-
-    def decay(c):
-        return ee[Q - 1 : Q, cols(c)]
-
-    def forward_step(c):
-        @pl.when(s == 0)
-        def _():
-            stt[c] = jnp.zeros((N, CW), BF)
-            fout[c] = car[:, cols(c)]
-
-        @pl.when(s > 0)
-        def _():
-            remote(fout.at[c], fin.at[c], f_send.at[c], f_recv.at[c], nxt).wait_recv()
-            state = keep * fin[c]
-            stt[c] = state.astype(BF)
-            fout[c] = decay(c) * state + car[:, cols(c)]
-
-        @pl.when(s < 7)
-        def _():
-            remote(fout.at[c], fin.at[c], f_send.at[c], f_recv.at[c], nxt).start()
+    HW = CW // 2
+    halves = [[slice(c * CW + k * HW, c * CW + (k + 1) * HW) for c in range(CH)] for k in range(2)]
+    my_half = pl.ds(pl.multiple_of(core * HW, HW), HW)
+    row8 = lax.broadcasted_iota(jnp.int32, (8, HW), 0)
+    row16 = lax.broadcasted_iota(jnp.int32, (16, HW), 0)
+    for c in range(CH):
+        part = mm(bm, win[:, cols(c)], 0, 0)
+        for k in range(2):
+            cx[k, c, 0:N, :] = part[:, k * HW : (k + 1) * HW]
+            gain = jnp.broadcast_to(ee[Q - 1 : Q, halves[k][c]], (8, HW))
+            cx[k, c, N : N + 8, :] = jnp.where(row8 == 0, gain, keep)
+
+    def first(a, b):
+        return jnp.where(core == 0, a, b), jnp.where(core == 0, b, a)
+
+    def gains(c):
+        mine, its = cx[core, c, N : N + 8, :], cxr[c, N : N + 8, :]
+        (d0, d1), (k0, k1) = first(mine[0:1], its[0:1]), first(mine[1:2], its[1:2])
+        return d0, d1, k0, k1
+
+    def message(ref, c, carry, gain):
+        up = gain.astype(BF).astype(F32)
+        ref[c, 0:N, :] = carry.astype(BF)
+        ref[c, N : N + 16, :] = jnp.where(row16 == 0, up, jnp.where(row16 == 1, gain - up, 0.0)).astype(BF)
+
+    def extend(ref, r, c, total):
+        g = ref[r - 1, c, N : N + 16, :].astype(F32)
+        return (g[0:1] + g[1:2]) * total + ref[r - 1, c, 0:N, :].astype(F32)
+
+    cx_copy = remote(cx.at[1 - core], cxr, cx_send.at[0], cx_recv.at[0], twin)
+    sx_copy = remote(sx, stt.at[:, :, my_half], sx_send.at[0], sx_recv.at[0], twin)
+
+    def f_copy(r):
+        return remote(fb, fbr.at[r - 1], f_send.at[r - 1], f_recv.at[r - 1], xdev(r))
+
+    def states_send():
+        cx_copy.wait_recv()
+        for c in range(CH):
+            d0, d1, k0, k1 = gains(c)
+            c0, c1 = first(cx[core, c, 0:N, :], cxr[c, 0:N, :])
+            message(fb, c, d1 * k1 * c0 + c1, d1 * k1 * d0 * k0)
+        for r in (1, 2, 3):
+
+            @pl.when(x + r < 4)
+            def _():
+                f_copy(r).start()
+
+    def states_done():
+        sacc[...] = jnp.zeros_like(sacc)
+        for r in (3, 2, 1):
+
+            @pl.when(x >= r)
+            def _():
+                f_copy(r).wait_recv()
+                for c in range(CH):
+                    sacc[c] = extend(fbr, r, c, sacc[c])
+
+        for c in range(CH):
+            d0, d1, k0, k1 = gains(c)
+            c0, c1 = first(cx[core, c, 0:N, :], cxr[c, 0:N, :])
+            st0 = k0 * sacc[c]
+            st1 = k1 * (d0 * st0 + c0)
+            mine, its = first(st0, st1)
+            stt[c, :, my_half] = mine.astype(BF)
+            sx[c] = its.astype(BF)
+        sx_copy.start()
+
+    def al_copy(c):
+        return remote(al.at[c, 1 - core], alr.at[c], al_send.at[c], al_recv.at[c], twin)
+
+    def a_copy(c, r):
+        return remote(ab.at[c], abr.at[r - 1, c], a_send.at[c, r - 1], a_recv.at[c, r - 1], xdev(4 - r))
+
+    def ax_copy(c):
+        return remote(ax.at[c], adt.at[c, :, my_half], ax_send.at[c], ax_recv.at[c], twin)
+
+    def adjoint_send(c):
+        al_copy(c).wait_recv()
+        d0, d1, k0, k1 = gains(c)
+        a0, a1 = first(al[c, core], alr[c])
+        message(ab, c, k0 * (d0 * k1 * a1 + a0), d1 * k1 * d0 * k0)
+        for r in (1, 2, 3):
+
+            @pl.when(x >= r)
+            def _():
+                a_copy(c, r).start()
+
+    def adjoint_done(c):
+        sacc[c] = jnp.zeros((N, HW), F32)
+        for r in (3, 2, 1):
+
+            @pl.when(x + r < 4)
+            def _():
+                a_copy(c, r).wait_recv()
+                sacc[c] = extend(abr, r, c, sacc[c])
+
+        d0, d1, k0, k1 = gains(c)
+        a0, a1 = first(al[c, core], alr[c])
+        ad1 = sacc[c]
+        mine, its = first(k1 * (d1 * ad1 + a1), ad1)
+        adt[c, :, my_half] = mine.astype(BF)
+        ax[c] = its.astype(BF)
+        ax_copy(c).start()
 
     scores = mm(cm, bm, 1, 1)
     ii = lax.broadcasted_iota(jnp.int32, (Q, Q), 0)
@@ -172,12 +260,6 @@
             cp.start()
             ozsends.append(cp)
 
-    intra(0)
-    intra(1)
-    share_og(0)
-    intra(2)
-    share_og(1)
-    intra(3)
 
     osends = []
 
@@ -189,21 +271,38 @@
         osends.append(cp)
 
     fsends = []
-
-    def share_w(c):
-        for r in (1, 3, 2):
-            frm = lax.rem(x + 4 - r, 4) * 2 + core
-            remote(w_ref.at[:, cols(c)], wb.at[c, frm], w_send.at[c, r - 1], w_recv.at[c, r - 1], xdev(r)).wait_recv()
-            cp = remote(wb.at[c, frm], wb.at[c, frm], wc_send.at[c, r], wc_recv.at[c, r], twin)
+    HR = 128
+
+    def chip(r):
+        return lax.rem(x + r, 4)
+
+    def wr_copy(c, k):
+        rows = pl.ds(k * HR, HR)
+        piece = wb.at[c, chip(3 if k == 0 else 1) * 2 + core, rows]
+        return remote(piece, piece, wr_send.at[c, k], wr_recv.at[c, k], xdev(1 if k == 0 else 3))
+
+    def relay_w(c):
+        for k, r in ((0, 1), (1, 3)):
+            w_copy(c, r).wait_recv()
+            cp = wr_copy(c, k)
             cp.start()
             fsends.append(cp)
+            cp = w_twin(c, 1 + k, chip(3 if k == 0 else 1) * 2 + core)
+            cp.start()
+            fsends.append(cp)
+
+    def share_w(c):
+        for k in range(2):
+            wr_copy(c, k).wait_recv()
+        cp = w_twin(c, 3, chip(2) * 2 + core)
+        cp.start()
+        fsends.append(cp)
 
     hsends = []
 
     def head(c):
-        for r in range(4):
-            frm = lax.rem(x + 4 - r, 4) * 2 + 1 - core
-            remote(wb.at[c, frm], wb.at[c, frm], wc_send.at[c, r], wc_recv.at[c, r], twin).wait_recv()
+        for j, r in enumerate((0, 3, 1, 2)):
+            w_twin(c, j, chip(r) * 2 + 1 - core).wait_recv()
         wmat = wb[c].reshape(8 * 256, CW)
         hs[c] = mm(oga[Q : 2 * Q, :], wmat).astype(BF)
         cp = remote(hs.at[c], hr.at[c], h_send.at[c], h_recv.at[c], partner)
@@ -217,24 +316,10 @@
         gg[:, cols(c)] = g
         wgc = (g.astype(F32) * ee[:, cols(c)]).astype(BF)
         wg[:, cols(c)] = wgc
-        adl[c] = mm(cm, wgc, 0, 0)
-
-    def backward_step(c):
-        @pl.when(s == 7)
-        def _():
-            adt[c] = jnp.zeros((N, CW), BF)
-            aout[c] = keep * adl[c]
-
-        @pl.when(s < 7)
-        def _():
-            remote(aout.at[c], ain.at[c], a_send.at[c], a_recv.at[c], prv).wait_recv()
-            back = ain[c]
-            adt[c] = back.astype(BF)
-            aout[c] = keep * (decay(c) * back + adl[c])
-
-        @pl.when(s > 0)
-        def _():
-            remote(aout.at[c], ain.at[c], a_send.at[c], a_recv.at[c], prv).start()
+        local = mm(cm, wgc, 0, 0)
+        for k in range(2):
+            al[c, k] = local[:, k * HW : (k + 1) * HW]
+        al_copy(c).start()
 
     def within_grads(c):
         gc = gg[:, cols(c)]
@@ -250,101 +335,167 @@
         gi[:, cols(c)] = acc
 
     def finish(c):
+        ax_copy(c).wait_recv()
         gin_ref[:, cols(c)] = (gi[:, cols(c)] + te[:, cols(c)] * mm(bm, adt[c])).astype(BF)
         nb = mm(win[:, cols(c)], adt[c], 1, 1)
         nc = mm(wg[:, cols(c)], stt[c], 1, 1)
         gb_ref[...] = nb if c == 0 else gb_ref[...] + nb
         gc_ref[...] = nc if c == 0 else gc_ref[...] + nc
 
-    dcsends, dxsends = [], []
+    dsends = []
+
+    def dc_copy(c, r):
+        return remote(ds.at[c, r], dr.at[c, r], dc_send.at[c, r], dc_recv.at[c, r], twin)
+
+    def da_copy(c, k):
+        return remote(
+            da.at[c, pl.ds(k * HR, HR)], dar.at[c, k], da_send.at[c, k], da_recv.at[c, k], xdev(1 if k == 0 else 3)
+        )
+
+    def db_copy(c, k):
+        return remote(db.at[c, k], dbr.at[c, k], db_send.at[c, k], db_recv.at[c, k], xdev(1 if k == 0 else 3))
+
+    def begin(cp):
+        cp.start()
+        dsends.append(cp)
 
     def weight_partial(c):
         remote(outs.at[c, pl.ds(0, Q), :], outs.at[c, pl.ds(Q, Q), :], o_send.at[c], o_recv.at[c], partner).wait_recv()
         oc = outs[c]
         for r in (2, 1, 3, 0):
-            other = lax.rem(x + r, 4) * 2 + 1 - core
-            ds[c, r] = mm(ogt[other], oc).astype(BF)
-            cp = remote(ds.at[c, r], dr.at[c, r], dc_send.at[c, r], dc_recv.at[c, r], twin)
-            cp.start()
-            dcsends.append(cp)
+            ds[c, r] = mm(ogt[chip(r) * 2 + 1 - core], oc).astype(BF)
+            begin(dc_copy(c, r))
 
     def weight_send(c):
         oc = outs[c]
         for r in (2, 1, 3, 0):
-            own = mm(ogt[lax.rem(x + r, 4) * 2 + core], oc)
-            remote(ds.at[c, r], dr.at[c, r], dc_send.at[c, r], dc_recv.at[c, r], twin).wait_recv()
+            own = mm(ogt[chip(r) * 2 + core], oc)
+            dc_copy(c, r).wait_recv()
             both = own + dr[c, r].astype(F32)
             if r == 0:
                 gw_ref[:, cols(c)] = both
+            elif r == 2:
+                da[c] = both.astype(BF)
+                begin(da_copy(c, 0))
+                begin(da_copy(c, 1))
             else:
-                dx[c, r - 1] = both.astype(BF)
-                cp = remote(dx.at[c, r - 1], dxr.at[c, r - 1], dx_send.at[c, r - 1], dx_recv.at[c, r - 1], xdev(r))
-                cp.start()
-                dxsends.append(cp)
+                dk[c, r // 2] = both
+
+    def weight_relay(c):
+        for k in range(2):
+            da_copy(c, k).wait_recv()
+            both, part = dk[c, k], dar[c, k].astype(F32)
+            rows = slice(k * HR, (k + 1) * HR)
+            rest = slice((1 - k) * HR, (2 - k) * HR)
+            db[c, k, rows, :] = (both[rows] + part).astype(BF)
+            db[c, k, rest, :] = both[rest].astype(BF)
+            begin(db_copy(c, k))
 
     def weight_sum(c):
         tot = gw_ref[:, cols(c)]
-        for r in range(1, 4):
-            remote(dx.at[c, r - 1], dxr.at[c, r - 1], dx_send.at[c, r - 1], dx_recv.at[c, r - 1], xdev(r)).wait_recv()
-            tot = tot + dxr[c, r - 1].astype(F32)
+        for k in range(2):
+            db_copy(c, k).wait_recv()
+            tot = tot + dbr[c, k].astype(F32)
         gw_ref[:, cols(c)] = tot
 
-    for c in range(CH):
-        forward_step(c)
-        output(c)
+    cx_copy.start()
+    intra(0)
+    states_send()
+    send_w(2)
+    send_w(3)
+    relay_w(0)
+    share_og(0)
+    intra(1)
+    relay_w(1)
+    share_og(1)
+    intra(2)
+    states_done()
+    relay_w(2)
+    intra(3)
+    sx_copy.wait_recv()
+    output(0)
+    output(1)
+    output(2)
+    output(3)
+    relay_w(3)
     for cp in locs:
         cp.wait()
     share_w(0)
+    share_w(1)
     for r in (1, 2, 3):
         frm = lax.rem(z + 4 - r, 4)
         for u in range(SUB):
             piece = oga.at[ogrows(frm, u), :]
             remote(piece, piece, oz_send.at[r - 1, u], oz_recv.at[r - 1, u], zdev(r)).wait_recv()
+    head(0)
     for k in range(8):
         ogt[k] = jnp.transpose(oga[:, k * 256 : (k + 1) * 256])
-    head(0)
-    share_w(1)
+    weight_partial(0)
     head(1)
-    weight_partial(0)
     share_w(2)
+    weight_partial(1)
+    weight_send(0)
     head(2)
-    weight_send(0)
-    weight_partial(1)
     share_w(3)
+    weight_partial(2)
+    weight_send(1)
+    weight_relay(0)
     head(3)
     head_grad(0)
-    weight_send(1)
-    backward_step(0)
+    weight_partial(3)
+    weight_send(2)
+    weight_relay(1)
     head_grad(1)
-    weight_partial(2)
-    backward_step(1)
+    adjoint_send(0)
+    weight_send(3)
+    weight_relay(2)
     head_grad(2)
-    weight_send(2)
-    backward_step(2)
-    weight_partial(3)
+    adjoint_send(1)
+    adjoint_done(0)
+    weight_relay(3)
     head_grad(3)
-    weight_send(3)
-    backward_step(3)
-    for c in range(CH):
-        within_grads(c)
-        finish(c)
+    adjoint_send(2)
+    adjoint_done(1)
+    within_grads(0)
+    adjoint_send(3)
+    adjoint_done(2)
+    within_grads(1)
+    finish(0)
+    adjoint_done(3)
+    within_grads(2)
+    finish(1)
+    within_grads(3)
+    finish(2)
+    finish(3)
     pb = psum[...].astype(BF)
     gb_ref[...] = gb_ref[...] + mm(pb, cm, 0, 0)
     gc_ref[...] = gc_ref[...] + mm(pb, bm)
     for c in range(CH):
         weight_sum(c)
 
-    for cp in wsends + oysends + ozsends + fsends + osends + hsends + dcsends + dxsends:
+    for cp in wsends + oysends + ozsends + fsends + osends + hsends + dsends:
         cp.wait_send()
+    cx_copy.wait_send()
+    sx_copy.wait_send()
     for c in range(CH):
-
-        @pl.when(s < 7)
+        al_copy(c).wait_send()
+        ax_copy(c).wait_send()
+    for r in (1, 2, 3):
+
+        @pl.when(x + r < 4)
         def _():
-            remote(fout.at[c], fin.at[c], f_send.at[c], f_recv.at[c], nxt).wait_send()
-
-        @pl.when(s > 0)
+            f_copy(r).wait_send()
+
+        @pl.when(x >= r)
         def _():
-            remote(aout.at[c], ain.at[c], a_send.at[c], a_recv.at[c], prv).wait_send()
+            for c in range(CH):
+                a_copy(c, r).wait_send()
+
+
+def hand_out(*refs):
+    n = len(refs) // 2
+    for k in range(n):
+        refs[n + k][...] = refs[k][...]
 
 
 def body(ssm_input, b_input, c_input, step_size, decay_rate, skip_gain, resets, out_grad, out_weight):
@@ -352,22 +503,28 @@
     width = HEADS * PS
     dma = pltpu.SemaphoreType.DMA
     v = pltpu.VMEM
+    HW = CW // 2
     scratch = [
         v((CH, 8, 256, CW), BF), v((2 * Q, 2048), BF), v((64, 2048), BF), v((8, 256, 2 * Q), BF),
         v((CH, HC * Q, CW), BF), v((HEADS, Q, Q), BF), v((HEADS, Q, Q), F32),
         v((Q, width), F32), v((Q, width), F32), v((Q, width), BF), v((Q, width), BF),
-        v((N, width), F32), v((CH, N, CW), F32), v((CH, N, CW), F32), v((CH, N, CW), BF),
+        v((CH, N, CW), BF), v((CH, N, CW), BF),
         v((Q, width), F32), v((CH, 2 * Q, CW), BF), v((CH, Q, CW), F32), v((CH, Q, CW), BF), v((CH, Q, CW), BF),
-        v((Q, width), BF), v((CH, N, CW), F32), v((CH, N, CW), F32), v((CH, N, CW), F32), v((CH, N, CW), BF),
-        v((Q, width), F32),
-        v((CH, 4, 256, CW), BF), v((CH, 4, 256, CW), BF), v((CH, 3, 256, CW), BF), v((CH, 3, 256, CW), BF),
+        v((Q, width), BF), v((Q, width), F32),
+        v((2, CH, N + 8, HW), F32), v((CH, N + 8, HW), F32), v((CH, N + 16, HW), BF), v((3, CH, N + 16, HW), BF),
+        v((CH, N, HW), F32), v((CH, N, HW), BF), v((CH, 2, N, HW), F32), v((CH, N, HW), F32),
+        v((CH, N + 16, HW), BF), v((3, CH, N + 16, HW), BF), v((CH, N, HW), BF),
+        v((CH, 4, 256, CW), BF), v((CH, 4, 256, CW), BF), v((CH, 256, CW), BF), v((CH, 2, 128, CW), BF),
+        v((CH, 2, 256, CW), F32), v((CH, 2, 256, CW), BF), v((CH, 2, 256, CW), BF),
         v((128, Q), F32), v((Q, 128), F32), v((Q, Q), F32),
-        dma((CH,)), dma((2, 8)), dma((CH, 3)), dma((CH, 3)), dma((CH, 4)), dma((CH, 4)), dma((SUB,)), dma((SUB,)),
-        dma((3, SUB)), dma((3, SUB)),
-        dma((CH,)), dma((CH,)), dma((CH,)), dma((CH,)), dma((CH,)), dma((CH,)), dma((CH,)), dma((CH,)),
-        dma((CH, 4)), dma((CH, 4)), dma((CH, 3)), dma((CH, 3)),
+        dma((CH,)), dma((2, 8)), dma((CH, 2)), dma((CH, 2)), dma((CH, 2)), dma((CH, 2)), dma((CH, 4)), dma((CH, 4)),
+        dma((SUB,)), dma((SUB,)), dma((3, SUB)), dma((3, SUB)),
+        dma((1,)), dma((1,)), dma((3,)), dma((3,)), dma((1,)), dma((1,)),
+        dma((CH,)), dma((CH,)), dma((CH, 3)), dma((CH, 3)), dma((CH,)), dma((CH,)),
+        dma((CH,)), dma((CH,)), dma((CH,)), dma((CH,)), dma((CH, 4)), dma((CH, 4)),
+        dma((CH, 2)), dma((CH, 2)), dma((CH, 2)), dma((CH, 2)),
     ]
-    gin, gb, gc, gw = pl.pallas_call(
+    results = pl.pallas_call(
         kernel,
         out_shape=(
             jax.ShapeDtypeStruct((Q, width), BF),
@@ -386,6 +543,15 @@
         ssm_input[0], b_input[0], c_input[0], step_size[0], decay_rate.reshape(1, HEADS),
         skip_gain.reshape(1, HEADS), resets, out_grad[0], out_weight,
     )
+    blocks = [pl.BlockSpec((64, a.shape[1]), lambda i: (i, 0)) for a in results]
+    gin, gb, gc, gw = pl.pallas_call(
+        hand_out,
+        out_shape=[jax.ShapeDtypeStruct(a.shape, a.dtype) for a in results],
+        grid=(4,),
+        in_specs=blocks,
+        out_specs=blocks,
+        name="hand_out",
+    )(*results)
     return gin[None], gb[None], gc[None], gw
 
 

time: 120 us -> 75.7 us (0.63)
  the two profiles are of different devices: /device:TPU:18 before, /device:TPU:1 now
where the time goes in v2:
time: 75.7 us; the launch traced here: 75.5 us
  Pallas kernels  74.1 us (98%)
  between operations  1.37 us (2%)
    pallas_call x1, Pallas kernels, body(): pl.pallas_call(kernel, out_shape=(jax.ShapeDtypeStruct((Q, width), BF), j...  70.3 us
    pallas_call x1, Pallas kernels, body(): pl.pallas_call(hand_out, out_shape=[jax.ShapeDtypeStruct(a.shape, a.dtype...  3.76 us

profile of v2, /device:TPU:1, one launch (start us, length us, event | category | flops | bytes accessed | tf_op | source)
XLA Modules:
  0.0 75.5 jit_solution(15894444096200978292)
XLA Ops:
  1.3 70.3 %block_backward.1 = (bf16[256,1024]{1,0:T(8,128)(2,1)}, f32[256,128]{1,0:T(8,128)}, f32[256,128]{1,0:T(8,128)}, f32[256,1024]{1,0:T(8,128)}) custom-call(bf16[256,1024]{1,0:T(8,128)(2,1)} %bitcast.11, bf16[256,128]{1,0:T(8,128)(2,1)} %bitcast.12, bf16[256,128]{1,0:T(8,128)(2,1)} %bitcast.13, f32[16,256]{1,0:T(8,128)} %bitcast.14, f32[1,16]{1,0:T(1,128)} %bitcast.15, ...), custom_call_target="tpu_custom_call" | custom-call | tf_op jit(solution)/shard_map/block_backward/pallas_call | solution.py:527
  71.6 3.8 %hand_out.1 = (bf16[256,1024]{1,0:T(8,128)(2,1)}, f32[256,128]{1,0:T(8,128)}, f32[256,128]{1,0:T(8,128)}, f32[256,1024]{1,0:T(8,128)}) custom-call(bf16[256,1024]{1,0:T(8,128)(2,1)} %get-tuple-element.12.refs_0_, f32[256,128]{1,0:T(8,128)} %get-tuple-element.13.refs_1_, f32[256,128]{1,0:T(8,128)} %get-tuple-element.14.refs_2_, ...), custom_call_target="tpu_custom_call" | custom-call | tf_op jit(solution)/shard_map/hand_out/pallas_call | solution.py:547

commit v3 on v2

--- a/solution.py
+++ b/solution.py
@@ -10,7 +10,7 @@
 F32 = jnp.float32
 Q, HEADS, PS, N = 256, 16, 64, 128
 CH, HC, CW = 4, 4, 256
-SUB = 2
+SUB = 4
 
 
 def mm(a, b, ca=1, cb=0, precision=None):
@@ -91,7 +91,6 @@
         cp.start()
         oysends.append(cp)
     send_w(0)
-    send_w(1)
     locs = []
     for c in range(CH):
         cp = pltpu.make_async_copy(w_ref.at[:, cols(c)], wb.at[c, s], loc_sem.at[c])
@@ -124,18 +123,23 @@
     keep = (1 - reset_ref[0, 0]).astype(F32)
 
     bm, cm = b_ref[...], c_ref[...]
-    win[...] = (x_ref[...].astype(F32) * te[...]).astype(BF)
     HW = CW // 2
     halves = [[slice(c * CW + k * HW, c * CW + (k + 1) * HW) for c in range(CH)] for k in range(2)]
     my_half = pl.ds(pl.multiple_of(core * HW, HW), HW)
     row8 = lax.broadcasted_iota(jnp.int32, (8, HW), 0)
     row16 = lax.broadcasted_iota(jnp.int32, (16, HW), 0)
-    for c in range(CH):
+
+    def cx_copy(c):
+        return remote(cx.at[1 - core, c], cxr.at[c], cx_send.at[c], cx_recv.at[c], twin)
+
+    def carry(c):
+        win[:, cols(c)] = (x_ref[:, cols(c)].astype(F32) * te[:, cols(c)]).astype(BF)
         part = mm(bm, win[:, cols(c)], 0, 0)
         for k in range(2):
             cx[k, c, 0:N, :] = part[:, k * HW : (k + 1) * HW]
             gain = jnp.broadcast_to(ee[Q - 1 : Q, halves[k][c]], (8, HW))
             cx[k, c, N : N + 8, :] = jnp.where(row8 == 0, gain, keep)
+        cx_copy(c).start()
 
     def first(a, b):
         return jnp.where(core == 0, a, b), jnp.where(core == 0, b, a)
@@ -154,43 +158,40 @@
         g = ref[r - 1, c, N : N + 16, :].astype(F32)
         return (g[0:1] + g[1:2]) * total + ref[r - 1, c, 0:N, :].astype(F32)
 
-    cx_copy = remote(cx.at[1 - core], cxr, cx_send.at[0], cx_recv.at[0], twin)
-    sx_copy = remote(sx, stt.at[:, :, my_half], sx_send.at[0], sx_recv.at[0], twin)
-
-    def f_copy(r):
-        return remote(fb, fbr.at[r - 1], f_send.at[r - 1], f_recv.at[r - 1], xdev(r))
-
-    def states_send():
-        cx_copy.wait_recv()
-        for c in range(CH):
-            d0, d1, k0, k1 = gains(c)
-            c0, c1 = first(cx[core, c, 0:N, :], cxr[c, 0:N, :])
-            message(fb, c, d1 * k1 * c0 + c1, d1 * k1 * d0 * k0)
+    def sx_copy(c):
+        return remote(sx.at[c], stt.at[c, :, my_half], sx_send.at[c], sx_recv.at[c], twin)
+
+    def f_copy(c, r):
+        return remote(fb.at[c], fbr.at[r - 1, c], f_send.at[c, r - 1], f_recv.at[c, r - 1], xdev(r))
+
+    def states_send(c):
+        cx_copy(c).wait_recv()
+        d0, d1, k0, k1 = gains(c)
+        c0, c1 = first(cx[core, c, 0:N, :], cxr[c, 0:N, :])
+        message(fb, c, d1 * k1 * c0 + c1, d1 * k1 * d0 * k0)
         for r in (1, 2, 3):
 
             @pl.when(x + r < 4)
             def _():
-                f_copy(r).start()
-
-    def states_done():
-        sacc[...] = jnp.zeros_like(sacc)
+                f_copy(c, r).start()
+
+    def states_done(c):
+        sacc[c] = jnp.zeros((N, HW), F32)
         for r in (3, 2, 1):
 
             @pl.when(x >= r)
             def _():
-                f_copy(r).wait_recv()
-                for c in range(CH):
-                    sacc[c] = extend(fbr, r, c, sacc[c])
-
-        for c in range(CH):
-            d0, d1, k0, k1 = gains(c)
-            c0, c1 = first(cx[core, c, 0:N, :], cxr[c, 0:N, :])
-            st0 = k0 * sacc[c]
-            st1 = k1 * (d0 * st0 + c0)
-            mine, its = first(st0, st1)
-            stt[c, :, my_half] = mine.astype(BF)
-            sx[c] = its.astype(BF)
-        sx_copy.start()
+                f_copy(c, r).wait_recv()
+                sacc[c] = extend(fbr, r, c, sacc[c])
+
+        d0, d1, k0, k1 = gains(c)
+        c0, c1 = first(cx[core, c, 0:N, :], cxr[c, 0:N, :])
+        st0 = k0 * sacc[c]
+        st1 = k1 * (d0 * st0 + c0)
+        mine, its = first(st0, st1)
+        stt[c, :, my_half] = mine.astype(BF)
+        sx[c] = its.astype(BF)
+        sx_copy(c).start()
 
     def al_copy(c):
         return remote(al.at[c, 1 - core], alr.at[c], al_send.at[c], al_recv.at[c], twin)
@@ -264,6 +265,7 @@
     osends = []
 
     def output(c):
+        sx_copy(c).wait_recv()
         o = yi[:, cols(c)] + ee[:, cols(c)] * mm(cm, stt[c])
         outs[c, 0:Q, :] = o.astype(BF)
         cp = remote(outs.at[c, pl.ds(0, Q), :], outs.at[c, pl.ds(Q, Q), :], o_send.at[c], o_recv.at[c], partner)
@@ -398,93 +400,105 @@
             tot = tot + dbr[c, k].astype(F32)
         gw_ref[:, cols(c)] = tot
 
-    cx_copy.start()
+    for c in range(CH):
+        carry(c)
+    states_send(0)
+    states_send(1)
+    states_send(2)
+    states_send(3)
     intra(0)
-    states_send()
+    share_og(0)
+    share_og(1)
+    send_w(1)
+    intra(1)
+    states_done(0)
+    relay_w(0)
+    share_og(2)
+    intra(2)
+    states_done(1)
     send_w(2)
+    output(0)
+    share_og(3)
+    intra(3)
+    states_done(2)
+    output(1)
+    states_done(3)
     send_w(3)
-    relay_w(0)
-    share_og(0)
-    intra(1)
-    relay_w(1)
-    share_og(1)
-    intra(2)
-    states_done()
-    relay_w(2)
-    intra(3)
-    sx_copy.wait_recv()
-    output(0)
-    output(1)
     output(2)
     output(3)
-    relay_w(3)
     for cp in locs:
         cp.wait()
     share_w(0)
-    share_w(1)
+    relay_w(1)
     for r in (1, 2, 3):
         frm = lax.rem(z + 4 - r, 4)
         for u in range(SUB):
             piece = oga.at[ogrows(frm, u), :]
             remote(piece, piece, oz_send.at[r - 1, u], oz_recv.at[r - 1, u], zdev(r)).wait_recv()
-    head(0)
     for k in range(8):
         ogt[k] = jnp.transpose(oga[:, k * 256 : (k + 1) * 256])
     weight_partial(0)
+    relay_w(2)
+    head(0)
+    weight_send(0)
+    relay_w(3)
+    share_w(1)
+    weight_partial(1)
     head(1)
-    share_w(2)
-    weight_partial(1)
-    weight_send(0)
-    head(2)
-    share_w(3)
-    weight_partial(2)
     weight_send(1)
     weight_relay(0)
-    head(3)
-    head_grad(0)
-    weight_partial(3)
+    share_w(2)
+    weight_partial(2)
+    head(2)
     weight_send(2)
     weight_relay(1)
-    head_grad(1)
+    share_w(3)
+    head(3)
+    weight_partial(3)
+    head_grad(0)
     adjoint_send(0)
     weight_send(3)
     weight_relay(2)
+    head_grad(1)
+    adjoint_send(1)
     head_grad(2)
-    adjoint_send(1)
     adjoint_done(0)
+    adjoint_send(2)
+    within_grads(0)
+    head_grad(3)
+    adjoint_send(3)
     weight_relay(3)
-    head_grad(3)
-    adjoint_send(2)
     adjoint_done(1)
-    within_grads(0)
-    adjoint_send(3)
+    finish(0)
+    within_grads(1)
     adjoint_done(2)
-    within_grads(1)
-    finish(0)
+    finish(1)
+    within_grads(2)
+    finish(2)
     adjoint_done(3)
-    within_grads(2)
-    finish(1)
     within_grads(3)
-    finish(2)
     finish(3)
+    weight_sum(0)
+    weight_sum(1)
     pb = psum[...].astype(BF)
     gb_ref[...] = gb_ref[...] + mm(pb, cm, 0, 0)
     gc_ref[...] = gc_ref[...] + mm(pb, bm)
-    for c in range(CH):
-        weight_sum(c)
+    weight_sum(2)
+    weight_sum(3)
 
     for cp in wsends + oysends + ozsends + fsends + osends + hsends + dsends:
         cp.wait_send()
-    cx_copy.wait_send()
-    sx_copy.wait_send()
     for c in range(CH):
+        cx_copy(c).wait_send()
+        sx_copy(c).wait_send()
         al_copy(c).wait_send()
         ax_copy(c).wait_send()
     for r in (1, 2, 3):
 
         @pl.when(x + r < 4)
         def _():
-            f_copy(r).wait_send()
+            for c in range(CH):
+                f_copy(c, r).wait_send()
 
         @pl.when(x >= r)
         def _():
@@ -493,9 +507,18 @@
 
 
 def hand_out(*refs):
-    n = len(refs) // 2
-    for k in range(n):
-        refs[n + k][...] = refs[k][...]
+    n = len(refs) // 3
+    src, dst, held, sem = refs[:n], refs[n : 2 * n], refs[2 * n : 3 * n], refs[3 * n]
+    parts = [(k, pl.ds(i * 64, 64), sem.at[:, k, i]) for k in range(n) for i in range(4)]
+    ins = [pltpu.make_async_copy(src[k].at[rows], held[k].at[rows], s.at[0]) for k, rows, s in parts]
+    outs = [pltpu.make_async_copy(held[k].at[rows], dst[k].at[rows], s.at[1]) for k, rows, s in parts]
+    for cp in ins:
+        cp.start()
+    for a, b in zip(ins, outs):
+        a.wait()
+        b.start()
+    for cp in outs:
+        cp.wait()
 
 
 def body(ssm_input, b_input, c_input, step_size, decay_rate, skip_gain, resets, out_grad, out_weight):
@@ -519,7 +542,7 @@
         v((128, Q), F32), v((Q, 128), F32), v((Q, Q), F32),
         dma((CH,)), dma((2, 8)), dma((CH, 2)), dma((CH, 2)), dma((CH, 2)), dma((CH, 2)), dma((CH, 4)), dma((CH, 4)),
         dma((SUB,)), dma((SUB,)), dma((3, SUB)), dma((3, SUB)),
-        dma((1,)), dma((1,)), dma((3,)), dma((3,)), dma((1,)), dma((1,)),
+        dma((CH,)), dma((CH,)), dma((CH, 3)), dma((CH, 3)), dma((CH,)), dma((CH,)),
         dma((CH,)), dma((CH,)), dma((CH, 3)), dma((CH, 3)), dma((CH,)), dma((CH,)),
         dma((CH,)), dma((CH,)), dma((CH,)), dma((CH,)), dma((CH, 4)), dma((CH, 4)),
         dma((CH, 2)), dma((CH, 2)), dma((CH, 2)), dma((CH, 2)),
@@ -543,13 +566,12 @@
         ssm_input[0], b_input[0], c_input[0], step_size[0], decay_rate.reshape(1, HEADS),
         skip_gain.reshape(1, HEADS), resets, out_grad[0], out_weight,
     )
-    blocks = [pl.BlockSpec((64, a.shape[1]), lambda i: (i, 0)) for a in results]
     gin, gb, gc, gw = pl.pallas_call(
         hand_out,
         out_shape=[jax.ShapeDtypeStruct(a.shape, a.dtype) for a in results],
-        grid=(4,),
-        in_specs=blocks,
-        out_specs=blocks,
+        in_specs=[anym] * 4,
+        out_specs=[anym] * 4,
+        scratch_shapes=[v(a.shape, a.dtype) for a in results] + [dma((2, 4, 4))],
         name="hand_out",
     )(*results)
     return gin[None], gb[None], gc[None], gw

time: 75.7 us -> 69.3 us (0.915)
  Pallas kernels: 74.1 us -> 67.6 us
    pallas_call x1, Pallas kernels: 70.3 us -> 65.1 us  [body(): pl.pallas_call(kernel, out_shape=(jax.ShapeDtypeStruct((Q, width), BF), j...]
    pallas_call x1, Pallas kernels: 3.76 us -> 2.56 us  [body(): pl.pallas_call(hand_out, out_shape=[jax.ShapeDtypeStruct(a.shape, a.dtype...]
where the time goes in v3:
time: 69.3 us; the launch traced here: 69.1 us
  Pallas kernels  67.6 us (98%)
  between operations  1.45 us (2%)
    pallas_call x1, Pallas kernels, body(): pl.pallas_call(kernel, out_shape=(jax.ShapeDtypeStruct((Q, width), BF), j...  65.1 us
    pallas_call x1, Pallas kernels, body(): pl.pallas_call(hand_out, out_shape=[jax.ShapeDtypeStruct(a.shape, a.dtype...  2.56 us

profile of v3, /device:TPU:1, one launch (start us, length us, event | category | flops | bytes accessed | tf_op | source)
XLA Modules:
  0.0 69.1 jit_solution(15369896304583294943)
XLA Ops:
  1.3 65.1 %block_backward.1 = (bf16[256,1024]{1,0:T(8,128)(2,1)}, f32[256,128]{1,0:T(8,128)}, f32[256,128]{1,0:T(8,128)}, f32[256,1024]{1,0:T(8,128)}) custom-call(bf16[256,1024]{1,0:T(8,128)(2,1)} %bitcast.11, bf16[256,128]{1,0:T(8,128)(2,1)} %bitcast.12, bf16[256,128]{1,0:T(8,128)(2,1)} %bitcast.13, f32[16,256]{1,0:T(8,128)} %bitcast.14, f32[1,16]{1,0:T(1,128)} %bitcast.15, ...), custom_call_target="tpu_custom_call" | custom-call | tf_op jit(solution)/shard_map/block_backward/pallas_call | solution.py:550
  66.3 2.6 %hand_out.1 = (bf16[256,1024]{1,0:T(8,128)(2,1)}, f32[256,128]{1,0:T(8,128)}, f32[256,128]{1,0:T(8,128)}, f32[256,1024]{1,0:T(8,128)}) custom-call(bf16[256,1024]{1,0:T(8,128)(2,1)} %get-tuple-element.12.refs_0_, f32[256,128]{1,0:T(8,128)} %get-tuple-element.13.refs_1_, f32[256,128]{1,0:T(8,128)} %get-tuple-element.14.refs_2_, ...), custom_call_target="tpu_custom_call" | custom-call | tf_op jit(solution)/shard_map/hand_out/pallas_call | solution.py:569

commit v4 on v3

--- a/solution.py
+++ b/solution.py
@@ -46,7 +46,6 @@
     peers = [xdev(1), xdev(2), xdev(3), zdev(1), zdev(2), zdev(3), twin, partner]
     for p in peers:
         pl.semaphore_signal(bar, inc=1, device_id=p, device_id_type=MESH)
-    pl.semaphore_wait(bar, len(peers))
 
     def remote(src, dst, ssem, rsem, dev):
         return pltpu.make_async_remote_copy(
@@ -78,19 +77,11 @@
             cp.start()
             wsends.append(cp)
 
-    for cp in ogl:
-        cp.wait()
     RS = 64 // SUB
 
     def ogrows(zz, u):
         return pl.ds(Q + zz * 64 + u * RS, RS)
 
-    oysends = []
-    for u in range(SUB):
-        cp = remote(ogs.at[pl.ds(u * RS, RS), :], oga.at[ogrows(z, u), :], oy_send.at[u], oy_recv.at[u], partner)
-        cp.start()
-        oysends.append(cp)
-    send_w(0)
     locs = []
     for c in range(CH):
         cp = pltpu.make_async_copy(w_ref.at[:, cols(c)], wb.at[c, s], loc_sem.at[c])
@@ -139,7 +130,6 @@
             cx[k, c, 0:N, :] = part[:, k * HW : (k + 1) * HW]
             gain = jnp.broadcast_to(ee[Q - 1 : Q, halves[k][c]], (8, HW))
             cx[k, c, N : N + 8, :] = jnp.where(row8 == 0, gain, keep)
-        cx_copy(c).start()
 
     def first(a, b):
         return jnp.where(core == 0, a, b), jnp.where(core == 0, b, a)
@@ -361,17 +351,26 @@
         cp.start()
         dsends.append(cp)
 
+    def turn(k):
+        ogt[k, :, Q : 2 * Q] = jnp.transpose(oga[Q : 2 * Q, pl.ds(pl.multiple_of(k * 256, 256), 256)])
+
     def weight_partial(c):
         remote(outs.at[c, pl.ds(0, Q), :], outs.at[c, pl.ds(Q, Q), :], o_send.at[c], o_recv.at[c], partner).wait_recv()
         oc = outs[c]
         for r in (2, 1, 3, 0):
-            ds[c, r] = mm(ogt[chip(r) * 2 + 1 - core], oc).astype(BF)
+            block = chip(r) * 2 + 1 - core
+            if c == 0:
+                turn(block)
+            ds[c, r] = mm(ogt[block], oc).astype(BF)
             begin(dc_copy(c, r))
 
     def weight_send(c):
         oc = outs[c]
         for r in (2, 1, 3, 0):
-            own = mm(ogt[chip(r) * 2 + core], oc)
+            block = chip(r) * 2 + core
+            if c == 0:
+                turn(block)
+            own = mm(ogt[block], oc)
             dc_copy(c, r).wait_recv()
             both = own + dr[c, r].astype(F32)
             if r == 0:
@@ -402,6 +401,17 @@
 
     for c in range(CH):
         carry(c)
+    pl.semaphore_wait(bar, len(peers))
+    for c in range(CH):
+        cx_copy(c).start()
+    for cp in ogl:
+        cp.wait()
+    oysends = []
+    for u in range(SUB):
+        cp = remote(ogs.at[pl.ds(u * RS, RS), :], oga.at[ogrows(z, u), :], oy_send.at[u], oy_recv.at[u], partner)
+        cp.start()
+        oysends.append(cp)
+    send_w(0)
     states_send(0)
     states_send(1)
     states_send(2)
@@ -428,6 +438,8 @@
     output(3)
     for cp in locs:
         cp.wait()
+    for k in range(8):
+        ogt[k, :, 0:Q] = jnp.transpose(oga[0:Q, k * 256 : (k + 1) * 256])
     share_w(0)
     relay_w(1)
     for r in (1, 2, 3):
@@ -435,8 +447,6 @@
         for u in range(SUB):
             piece = oga.at[ogrows(frm, u), :]
             remote(piece, piece, oz_send.at[r - 1, u], oz_recv.at[r - 1, u], zdev(r)).wait_recv()
-    for k in range(8):
-        ogt[k] = jnp.transpose(oga[:, k * 256 : (k + 1) * 256])
     weight_partial(0)
     relay_w(2)
     head(0)

time: 69.3 us -> 67 us (0.967)
  Pallas kernels: 67.6 us -> 65.4 us
    pallas_call x1, Pallas kernels: 65.1 us -> 62.9 us  [body(): pl.pallas_call(kernel, out_shape=(jax.ShapeDtypeStruct((Q, width), BF), j...]
where the time goes in v4:
time: 67 us; the launch traced here: 66.9 us
  Pallas kernels  65.4 us (98%)
  between operations  1.45 us (2%)
    pallas_call x1, Pallas kernels, body(): pl.pallas_call(kernel, out_shape=(jax.ShapeDtypeStruct((Q, width), BF), j...  62.9 us
    pallas_call x1, Pallas kernels, body(): pl.pallas_call(hand_out, out_shape=[jax.ShapeDtypeStruct(a.shape, a.dtype...  2.56 us

profile of v4, /device:TPU:1, one launch (start us, length us, event | category | flops | bytes accessed | tf_op | source)
XLA Modules:
  0.0 66.9 jit_solution(10169341548979631371)
XLA Ops:
  1.3 62.9 %block_backward.1 = (bf16[256,1024]{1,0:T(8,128)(2,1)}, f32[256,128]{1,0:T(8,128)}, f32[256,128]{1,0:T(8,128)}, f32[256,1024]{1,0:T(8,128)}) custom-call(bf16[256,1024]{1,0:T(8,128)(2,1)} %bitcast.11, bf16[256,128]{1,0:T(8,128)(2,1)} %bitcast.12, bf16[256,128]{1,0:T(8,128)(2,1)} %bitcast.13, f32[16,256]{1,0:T(8,128)} %bitcast.14, f32[1,16]{1,0:T(1,128)} %bitcast.15, ...), custom_call_target="tpu_custom_call" | custom-call | tf_op jit(solution)/shard_map/block_backward/pallas_call | solution.py:560
  64.2 2.6 %hand_out.1 = (bf16[256,1024]{1,0:T(8,128)(2,1)}, f32[256,128]{1,0:T(8,128)}, f32[256,128]{1,0:T(8,128)}, f32[256,1024]{1,0:T(8,128)}) custom-call(bf16[256,1024]{1,0:T(8,128)(2,1)} %get-tuple-element.12.refs_0_, f32[256,128]{1,0:T(8,128)} %get-tuple-element.13.refs_1_, f32[256,128]{1,0:T(8,128)} %get-tuple-element.14.refs_2_, ...), custom_call_target="tpu_custom_call" | custom-call | tf_op jit(solution)/shard_map/hand_out/pallas_call | solution.py:579

commit v5 on v4

--- a/solution.py
+++ b/solution.py
@@ -471,16 +471,16 @@
     weight_relay(2)
     head_grad(1)
     adjoint_send(1)
+    within_grads(0)
     head_grad(2)
     adjoint_done(0)
     adjoint_send(2)
-    within_grads(0)
+    within_grads(1)
     head_grad(3)
     adjoint_send(3)
     weight_relay(3)
     adjoint_done(1)
     finish(0)
-    within_grads(1)
     adjoint_done(2)
     finish(1)
     within_grads(2)

time: 67 us -> 66.9 us (level)
  no operation moved by 1% of the time
where the time goes in v5:
time: 66.9 us; the launch traced here: 66.8 us
  Pallas kernels  65.3 us (98%)
  between operations  1.45 us (2%)
    pallas_call x1, Pallas kernels, body(): pl.pallas_call(kernel, out_shape=(jax.ShapeDtypeStruct((Q, width), BF), j...  62.7 us
    pallas_call x1, Pallas kernels, body(): pl.pallas_call(hand_out, out_shape=[jax.ShapeDtypeStruct(a.shape, a.dtype...  2.56 us

profile of v5, /device:TPU:1, one launch (start us, length us, event | category | flops | bytes accessed | tf_op | source)
XLA Modules:
  0.0 66.8 jit_solution(5322939169683915171)
XLA Ops:
  1.3 62.7 %block_backward.1 = (bf16[256,1024]{1,0:T(8,128)(2,1)}, f32[256,128]{1,0:T(8,128)}, f32[256,128]{1,0:T(8,128)}, f32[256,1024]{1,0:T(8,128)}) custom-call(bf16[256,1024]{1,0:T(8,128)(2,1)} %bitcast.11, bf16[256,128]{1,0:T(8,128)(2,1)} %bitcast.12, bf16[256,128]{1,0:T(8,128)(2,1)} %bitcast.13, f32[16,256]{1,0:T(8,128)} %bitcast.14, f32[1,16]{1,0:T(1,128)} %bitcast.15, ...), custom_call_target="tpu_custom_call" | custom-call | tf_op jit(solution)/shard_map/block_backward/pallas_call | solution.py:560
  64.0 2.6 %hand_out.1 = (bf16[256,1024]{1,0:T(8,128)(2,1)}, f32[256,128]{1,0:T(8,128)}, f32[256,128]{1,0:T(8,128)}, f32[256,1024]{1,0:T(8,128)}) custom-call(bf16[256,1024]{1,0:T(8,128)(2,1)} %get-tuple-element.12.refs_0_, f32[256,128]{1,0:T(8,128)} %get-tuple-element.13.refs_1_, f32[256,128]{1,0:T(8,128)} %get-tuple-element.14.refs_2_, ...), custom_call_target="tpu_custom_call" | custom-call | tf_op jit(solution)/shard_map/hand_out/pallas_call | solution.py:579
